TPU v7x, 32 devices: a whole 2x2x4 slice. The times are simulated.
32 devices in a mesh: groups: 2 (over y), seq: 4 (over z), head: 2 (over x), prompt: 2 (over core).
Axes of the slice: x: 2, y: 2, z: 4, core: 2. Of those that a mesh axis runs over, the one named last changes fastest.
Arguments:
- prompt_queries: bfloat16 [4, 512, 2048], P(('groups', 'prompt'), 'seq', 'head'), parts along dimension 0, may hold values from -6 to 6
- prompt_keys: bfloat16 [4, 512, 2048], P(('groups', 'prompt'), 'seq', 'head'), parts along dimension 0, may hold values from -20 to 20
- prompt_values: bfloat16 [4, 512, 4096], P(('groups', 'prompt'), 'seq', 'head'), parts along dimension 0, may hold values from -6 to 6
- prompt_beta: float32 [4, 32, 512], P(('groups', 'prompt'), 'head', 'seq'), parts along dimension 0, may hold values from 0.005 to 0.15
- prompt_decay: float32 [4, 32, 512], P(('groups', 'prompt'), 'head', 'seq'), parts along dimension 0, may hold values from -0.7 to 0
- suffix_queries: bfloat16 [32, 256, 2048], P(('groups', 'seq', 'prompt'), None, 'head'), parts along dimension 0, may hold values from -6 to 6
- suffix_keys: bfloat16 [32, 256, 2048], P(('groups', 'seq', 'prompt'), None, 'head'), parts along dimension 0, may hold values from -20 to 20
- suffix_values: bfloat16 [32, 256, 4096], P(('groups', 'seq', 'prompt'), None, 'head'), parts along dimension 0, may hold values from -6 to 6
- suffix_beta: float32 [32, 32, 256], P(('groups', 'seq', 'prompt'), 'head'), parts along dimension 0, may hold values from 0.005 to 0.15
- suffix_decay: float32 [32, 32, 256], P(('groups', 'seq', 'prompt'), 'head'), parts along dimension 0, may hold values from -0.2 to 0
- norm_gain: float32 [128], replicated, may hold values from 0.25 to 1.75
- slot_branch: int32 [32], P('groups'), parts along dimension 0, may hold values from 0 to 15, each once
- branch_length: int32 [32], P('groups'), parts along dimension 0, may hold values from 1 to 256, 2048 in all
- branch_prompt: int32 [32], P('groups'), parts along dimension 0, may hold values from 0 to 1
Outputs:
- prompt_out: bfloat16 [4, 512, 4096], P(('groups', 'prompt'), 'seq', 'head'), parts along dimension 0
- suffix_out: bfloat16 [32, 256, 4096], P(('groups', 'seq', 'prompt'), None, 'head'), parts along dimension 0
There are 2 independent parts, one for each index of `groups`. A program takes and returns all parts, laid end to end along the dimension named above; an argument that names none is the same for every part. Nothing has to cross between parts.
Inputs may be any that keep to these rules, and one draw needn't show every extreme that they name: slot_branch names every branch exactly once. `branch_length`: the lengths sum to 2048 and one of them is exactly 256.
All inputs are finite; a program needn't handle non-finite values.
Results may differ from a plain program's by a relative error of at most 0.0067.
Values sent between devices are 32-bit elements; how exact they have to be, the bound alone decides.
A program may use at most 128 MiB of HBM per device.

v0:
```python
import functools

import jax
import jax.numpy as jnp
from jax import lax
from jax.experimental import pallas as pl
from jax.experimental.pallas import tpu as pltpu
from jax.sharding import PartitionSpec as P

DK = 128
DV = 128
CH = 128
EPS_NORM = 1e-06
F32 = jnp.float32
BF16 = jnp.bfloat16
NN = (((1,), (0,)), ((), ()))
NT = (((1,), (1,)), ((), ()))
TN = (((0,), (0,)), ((), ()))


def mm(a, b, dims=NN):
    return lax.dot_general(a, b, dims, preferred_element_type=F32)


def unit(x):
    w = x.astype(F32)
    return (w * lax.rsqrt(jnp.sum(w * w, axis=-1, keepdims=True) + EPS_NORM)).astype(BF16)


def iotas():
    return (
        lax.broadcasted_iota(jnp.int32, (CH, CH), 0),
        lax.broadcasted_iota(jnp.int32, (CH, CH), 1),
    )


def running_log(decay):
    rows, cols = iotas()
    tri = jnp.where(rows <= cols, 1.0, 0.0).astype(F32)
    return lax.dot_general(
        decay, tri, NN, precision=lax.Precision.HIGHEST, preferred_element_type=F32
    )


def pre_kernel(rep, q_ref, k_ref, beta_ref, decay_ref, qk_ref, solve_ref, gram_ref):
    key_heads = q_ref.shape[2] // DK
    heads = key_heads * rep
    rows, cols = iotas()
    upto = rows >= cols
    strict = rows > cols
    apart = rows ^ cols
    log_row = running_log(decay_ref[0])
    log_col = log_row.T
    beta_row = beta_ref[0]
    beta_col = beta_row.T
    lower = []
    for j in range(key_heads):
        q = unit(q_ref[0, :, j * DK : (j + 1) * DK])
        k = unit(k_ref[0, :, j * DK : (j + 1) * DK])
        qk_ref[0, 0, j, :CH, :] = q
        qk_ref[0, 0, j, CH:, :] = k
        grams = mm(jnp.concatenate([q, k], axis=0), k, NT)
        for r in range(rep):
            h = j * rep + r
            spread = log_col[:, h : h + 1] - log_row[h : h + 1, :]
            ratio = jnp.exp(jnp.where(upto, spread, -1e30))
            gram_ref[0, 0, h] = (grams[:CH] * ratio).astype(BF16)
            lower.append(jnp.where(strict, beta_col[:, h : h + 1] * ratio * grams[CH:], 0.0))
    eye = jnp.where(rows == cols, 1.0, 0.0).astype(F32)
    first = strict & (apart == 1)
    inv = [eye - jnp.where(first, low, 0.0) for low in lower]
    level = 1
    while (1 << level) < CH:
        pick = strict & ((apart >> level) == 1)
        inv16 = [t.astype(BF16) for t in inv]
        mid = [mm(jnp.where(pick, low, 0.0).astype(BF16), t) for low, t in zip(lower, inv16)]
        inv = [t - mm(t16, x.astype(BF16)) for t, t16, x in zip(inv, inv16, mid)]
        level += 1
    for h in range(heads):
        off = jnp.where(strict, inv[h], 0.0) * beta_row[h : h + 1, :]
        solve_ref[0, 0, h] = off.astype(BF16)


def advance(qk, vals, solve, gram, logs, beta_cols, states):
    reads = mm(qk, jnp.concatenate([s.astype(BF16) for s in states], axis=1))
    outs, tails = [], []
    for r, state in enumerate(states):
        fade = jnp.exp(logs[r])
        part = reads[:, r * DV : (r + 1) * DV]
        resid = vals[r].astype(F32) - fade * part[CH:]
        new = beta_cols[r] * resid + mm(solve[r], resid.astype(BF16))
        outs.append(fade * part[:CH] + mm(gram[r], new.astype(BF16)))
        tails.append((jnp.exp(logs[r][CH - 1 :, :] - logs[r]) * new).astype(BF16))
    grown = mm(qk[CH:], jnp.concatenate(tails, axis=1), TN)
    states = [
        jnp.exp(logs[r][CH - 1 :, :]) * s + grown[:, r * DV : (r + 1) * DV]
        for r, s in enumerate(states)
    ]
    return outs, states


def norm_rows(o, gain):
    return o * lax.rsqrt(jnp.mean(o * o, axis=-1, keepdims=True) + EPS_NORM) * gain


def seq_kernel(
    rep, keep, owner_ref, length_ref, qk_ref, v_ref, solve_ref, gram_ref,
    beta_ref, decay_ref, seed_ref, gain_ref, out_ref, *end_ref
):
    spans, key_heads = qk_ref.shape[1], qk_ref.shape[2]
    heads = key_heads * rep
    length = length_ref[pl.program_id(0)]
    gain = gain_ref[...]
    states = [seed_ref[0, h] for h in range(heads)]
    place = lax.broadcasted_iota(jnp.int32, (CH, DV), 0)
    for c in range(spans):
        span = slice(c * CH, (c + 1) * CH)
        log_col = running_log(decay_ref[0, :, span]).T
        beta_col = beta_ref[0, :, span].T
        live = place + c * CH < length
        for j in range(key_heads):
            hs = range(j * rep, (j + 1) * rep)
            outs, grown = advance(
                qk_ref[0, c, j],
                [v_ref[0, span, h * DV : (h + 1) * DV] for h in hs],
                [solve_ref[0, c, h] for h in hs],
                [gram_ref[0, c, h] for h in hs],
                [log_col[:, h : h + 1] for h in hs],
                [beta_col[:, h : h + 1] for h in hs],
                [states[h] for h in hs],
            )
            for h, o, s in zip(hs, outs, grown):
                states[h] = s
                out_ref[0, span, h * DV : (h + 1) * DV] = jnp.where(
                    live, norm_rows(o, gain), 0.0
                ).astype(BF16)
    if keep:
        for h in range(heads):
            end_ref[0][0, h] = states[h]


def group_of(key_heads):
    return 4 if key_heads % 4 == 0 else key_heads


PARAMS = dict(vmem_limit_bytes=48 * 1024 * 1024)


def prepare(q, k, beta, decay):
    slots, tokens, width = q.shape
    key_heads, heads = width // DK, beta.shape[1]
    rep, g, spans = heads // key_heads, group_of(width // DK), tokens // CH
    gate = pl.BlockSpec((1, g * rep, CH), lambda s, c, j: (s, j, c))
    rows = pl.BlockSpec((1, CH, g * DK), lambda s, c, j: (s, c, j))
    square = pl.BlockSpec((1, 1, g * rep, CH, CH), lambda s, c, j: (s, c, j, 0, 0))
    return pl.pallas_call(
        functools.partial(pre_kernel, rep),
        grid=(slots, spans, key_heads // g),
        in_specs=[rows, rows, gate, gate],
        out_specs=[
            pl.BlockSpec((1, 1, g, 2 * CH, DK), lambda s, c, j: (s, c, j, 0, 0)),
            square,
            square,
        ],
        out_shape=[
            jax.ShapeDtypeStruct((slots, spans, key_heads, 2 * CH, DK), BF16),
            jax.ShapeDtypeStruct((slots, spans, heads, CH, CH), BF16),
            jax.ShapeDtypeStruct((slots, spans, heads, CH, CH), BF16),
        ],
        compiler_params=pltpu.CompilerParams(**PARAMS),
        cost_estimate=pl.CostEstimate(
            flops=slots * tokens * heads * CH * CH * 30, bytes_accessed=slots * tokens * heads * 800,
            transcendentals=slots * tokens * heads * CH,
        ),
        name="prepare",
    )(q, k, beta, decay)


def sweep(terms, v, beta, decay, seeds, owner, length, gain, keep):
    qk, solve, gram = terms
    slots, spans, key_heads = qk.shape[:3]
    heads = beta.shape[1]
    rep, g, tokens = heads // key_heads, group_of(key_heads), spans * CH
    gate = pl.BlockSpec((1, g * rep, tokens), lambda s, j, *_: (s, j, 0))
    vals = pl.BlockSpec((1, tokens, g * rep * DV), lambda s, j, *_: (s, 0, j))
    square = pl.BlockSpec((1, spans, g * rep, CH, CH), lambda s, j, *_: (s, 0, j, 0, 0))
    out_specs, out_shape = [vals], [jax.ShapeDtypeStruct(v.shape, BF16)]
    if keep:
        out_specs.append(pl.BlockSpec((1, g * rep, DK, DV), lambda s, j, *_: (s, j, 0, 0)))
        out_shape.append(jax.ShapeDtypeStruct((slots, heads, DK, DV), F32))
    return pl.pallas_call(
        functools.partial(seq_kernel, rep, keep),
        grid_spec=pltpu.PrefetchScalarGridSpec(
            num_scalar_prefetch=2,
            grid=(slots, key_heads // g),
            in_specs=[
                pl.BlockSpec((1, spans, g, 2 * CH, DK), lambda s, j, *_: (s, 0, j, 0, 0)),
                vals,
                square,
                square,
                gate,
                gate,
                pl.BlockSpec((1, g * rep, DK, DV), lambda s, j, own, _: (own[s], j, 0, 0)),
                pl.BlockSpec((1, DV), lambda s, j, *_: (0, 0)),
            ],
            out_specs=out_specs,
        ),
        out_shape=out_shape,
        compiler_params=pltpu.CompilerParams(**PARAMS),
        name="sweep",
    )(owner, length, qk, v, solve, gram, beta, decay, seeds, gain)


def from_behind(value, axis):
    count = lax.axis_size(axis)
    return lax.ppermute(value, axis, [(i, i + 1) for i in range(count - 1)])


def slot_facts(slot_branch, branch_length, branch_prompt, slot_count):
    rank = lax.axis_index("seq") * lax.axis_size("prompt") + lax.axis_index("prompt")
    slot_ids = rank * slot_count + jnp.arange(slot_count, dtype=jnp.int32)
    branch_ids = jnp.arange(slot_branch.shape[0], dtype=jnp.int32)
    mine = jnp.sum(
        jnp.where(slot_ids[:, None] == branch_ids[None, :], slot_branch[None, :], 0), axis=1
    )
    hit = mine[:, None] == branch_ids[None, :]
    length = jnp.sum(jnp.where(hit, branch_length[None, :], 0), axis=1)
    owner = jnp.sum(jnp.where(hit, branch_prompt[None, :], 0), axis=1)
    return length, owner


def local(
    prompt_queries, prompt_keys, prompt_values, prompt_beta, prompt_decay,
    suffix_queries, suffix_keys, suffix_values, suffix_beta, suffix_decay,
    norm_gain, slot_branch, branch_length, branch_prompt,
):
    gain = norm_gain[None, :]
    length, owner = slot_facts(slot_branch, branch_length, branch_prompt, suffix_queries.shape[0])
    terms = prepare(prompt_queries, prompt_keys, prompt_beta, prompt_decay)
    heads = prompt_beta.shape[1]
    whole = jnp.full((1,), prompt_queries.shape[1], jnp.int32)
    zero = jnp.zeros((1,), jnp.int32)
    state = jnp.zeros((1, heads, DK, DV), F32)
    count = lax.axis_size("seq")
    for step in range(count):
        prompt_out, state_out = sweep(
            terms, prompt_values, prompt_beta, prompt_decay, state, zero, whole, gain, True
        )
        if step < count - 1:
            state = from_behind(state_out, "seq")
    final = jnp.where(lax.axis_index("seq") == count - 1, state_out, 0.0)
    final = lax.psum(final, "seq")
    finals = lax.all_gather(final, "prompt", axis=0, tiled=True)
    suffix_terms = prepare(suffix_queries, suffix_keys, suffix_beta, suffix_decay)
    suffix_out = sweep(
        suffix_terms, suffix_values, suffix_beta, suffix_decay, finals, owner, length, gain, False
    )[0]
    return (prompt_out, suffix_out)


def solution(mesh):
    lead = P(("groups", "prompt"), "seq", "head")
    lead_gate = P(("groups", "prompt"), "head", "seq")
    slot = P(("groups", "seq", "prompt"), None, "head")
    slot_gate = P(("groups", "seq", "prompt"), "head", None)
    return jax.shard_map(
        local,
        mesh=mesh,
        in_specs=(
            lead, lead, lead, lead_gate, lead_gate, slot, slot, slot, slot_gate, slot_gate,
            P(), P("groups"), P("groups"), P("groups"),
        ),
        out_specs=(lead, slot),
        check_vma=False,
    )
```

profile of v0, /device:TPU:0, one launch (start us, length us, event | category | flops | bytes accessed | tf_op | source)
XLA Modules:
  0.0 225.0 jit_solution(15260293967407576975)
XLA Ops:
  7.2 0.0 copy-start
  7.2 0.0 all-reduce.2.cloned.1.call-start
  7.2 0.0 copy-start.4
  7.2 0.7 copy-done.4
  8.0 0.0 copy-start.6
  8.0 0.7 copy-done.6
  8.7 0.0 copy-start.13
  8.7 0.9 copy-done.13
  9.6 0.0 copy-start.14
  9.6 0.9 copy-done.14
  10.6 0.0 copy-start.5
  10.6 0.0 copy-start.10
  10.6 5.2 %prepare.2 = (bf16[1,1,8,256,128]{4,3,2,1,0:T(8,128)(2,1)S(1)}, bf16[1,1,16,128,128]{4,3,2,1,0:T(8,128)(2,1)S(1)}, bf16[1,1,16,128,128]{4,3,2,1,0:T(8,128)(2,1)S(1)}) custom-call(bf16[1,128,1024]{2,1,0:T(8,128)(2,1)S(1)} %copy-done.13, bf16[1,128,1024]{2,1,0:T(8,128)(2,1)S(1)} %copy-done.14, f32[1,16,128]{2,1,0:T(8,128)S(1)} %copy-done.4, ...), custom_call_target="tpu_custom_call" | custom-call | flops 1006632960 | bytes 1638400 | tf_op jit(solution)/shard_map/prepare/pallas_call | solution.py:156
  15.8 0.1 broadcast_in_dim.39.seed_ref
  15.9 0.0 copy-done
  15.9 0.0 copy-done.5
  15.9 0.0 copy-done.10
  15.9 5.5 %sweep.5 = (bf16[1,128,2048]{2,1,0:T(8,128)(2,1)}, f32[1,16,128,128]{3,2,1,0:T(8,128)S(1)}) custom-call(s32[1]{0:T(128)} %constant.9.clone.1.owner_ref, s32[1]{0:T(128)} %constant.3.clone.1.length_ref, bf16[1,1,8,256,128]{4,3,2,1,0:T(8,128)(2,1)S(1)} %get-tuple-element.13.qk_ref, bf16[1,128,2048]{2,1,0:T(8,128)(2,1)S(1)} %copy-done, ...), custom_call_target="tpu_custom_call" | custom-call | tf_op jit(solution)/shard_map/sweep/pallas_call | solution.py:191
  21.4 5.0 %collective-permute-start = (f32[1,16,128,128]{3,2,1,0:T(8,128)S(1)}, f32[1,16,128,128]{3,2,1,0:T(8,128)S(1)}, u32[]{:S(2)}, u32[]{:S(2)}) collective-permute-start(f32[1,16,128,128]{3,2,1,0:T(8,128)S(1)} %get-tuple-element.16), channel_id=1, source_target_pairs={{0,4},{4,8},{8,12},{1,5},{5,9},{9,13},{2,6},{6,10},{10,14},{3,7},{... | collective-permute-start | bytes 3145736 | tf_op jit(solution)/shard_map/ppermute | solution.py:216
  26.4 22.3 %collective-permute-done.seed_ref = f32[1,16,128,128]{3,2,1,0:T(8,128)S(1)} collective-permute-done((f32[1,16,128,128]{3,2,1,0:T(8,128)S(1)}, f32[1,16,128,128]{3,2,1,0:T(8,128)S(1)}, u32[]{:S(2)}, u32[]{:S(2)}) %collective-permute-start) | collective-permute-done | bytes 1048608 | tf_op jit(solution)/shard_map/ppermute | solution.py:216
  48.8 5.5 %sweep.6 = (bf16[1,128,2048]{2,1,0:T(8,128)(2,1)}, f32[1,16,128,128]{3,2,1,0:T(8,128)S(1)}) custom-call(s32[1]{0:T(128)} %constant.9.clone.1.owner_ref, s32[1]{0:T(128)} %constant.3.clone.1.length_ref, bf16[1,1,8,256,128]{4,3,2,1,0:T(8,128)(2,1)S(1)} %get-tuple-element.13.qk_ref, bf16[1,128,2048]{2,1,0:T(8,128)(2,1)S(1)} %copy-done, ...), custom_call_target="tpu_custom_call" | custom-call | tf_op jit(solution)/shard_map/sweep/pallas_call | solution.py:191
  54.3 0.0 copy-start.7
  54.3 4.6 %collective-permute-start.1 = (f32[1,16,128,128]{3,2,1,0:T(8,128)S(1)}, f32[1,16,128,128]{3,2,1,0:T(8,128)S(1)}, u32[]{:S(2)}, u32[]{:S(2)}) collective-permute-start(f32[1,16,128,128]{3,2,1,0:T(8,128)S(1)} %get-tuple-element.17), channel_id=1, source_target_pairs={{0,4},{4,8},{8,12},{1,5},{5,9},{9,13},{2,6},{6,10},{10,14},{3,7},{... | collective-permute-start | bytes 3145736 | tf_op jit(solution)/shard_map/ppermute | solution.py:216
  58.8 21.5 %collective-permute-done.1.seed_ref = f32[1,16,128,128]{3,2,1,0:T(8,128)S(1)} collective-permute-done((f32[1,16,128,128]{3,2,1,0:T(8,128)S(1)}, f32[1,16,128,128]{3,2,1,0:T(8,128)S(1)}, u32[]{:S(2)}, u32[]{:S(2)}) %collective-permute-start.1) | collective-permute-done | bytes 1048608 | tf_op jit(solution)/shard_map/ppermute | solution.py:216
  80.3 5.6 %sweep.7 = (bf16[1,128,2048]{2,1,0:T(8,128)(2,1)}, f32[1,16,128,128]{3,2,1,0:T(8,128)}) custom-call(s32[1]{0:T(128)} %constant.9.clone.1.owner_ref, s32[1]{0:T(128)} %constant.3.clone.1.length_ref, bf16[1,1,8,256,128]{4,3,2,1,0:T(8,128)(2,1)S(1)} %get-tuple-element.13.qk_ref, bf16[1,128,2048]{2,1,0:T(8,128)(2,1)S(1)} %copy-done, ...), custom_call_target="tpu_custom_call" | custom-call | tf_op jit(solution)/shard_map/sweep/pallas_call | solution.py:191
  85.9 4.4 %collective-permute-start.2 = (f32[1,16,128,128]{3,2,1,0:T(8,128)}, f32[1,16,128,128]{3,2,1,0:T(8,128)S(1)}, u32[]{:S(2)}, u32[]{:S(2)}) collective-permute-start(f32[1,16,128,128]{3,2,1,0:T(8,128)} %get-tuple-element.18), channel_id=1, source_target_pairs={{0,4},{4,8},{8,12},{1,5},{5,9},{9,13},{2,6},{6,10},{10,14},{3,7},{... | collective-permute-start | bytes 3145736 | tf_op jit(solution)/shard_map/ppermute | solution.py:216
  90.4 20.8 %collective-permute-done.2.seed_ref = f32[1,16,128,128]{3,2,1,0:T(8,128)S(1)} collective-permute-done((f32[1,16,128,128]{3,2,1,0:T(8,128)}, f32[1,16,128,128]{3,2,1,0:T(8,128)S(1)}, u32[]{:S(2)}, u32[]{:S(2)}) %collective-permute-start.2) | collective-permute-done | bytes 1048608 | tf_op jit(solution)/shard_map/ppermute | solution.py:216
  111.2 0.0 copy-done.7
  111.2 5.5 %sweep.8 = (bf16[1,128,2048]{2,1,0:T(8,128)(2,1)}, f32[1,16,128,128]{3,2,1,0:T(8,128)S(1)}) custom-call(s32[1]{0:T(128)} %constant.9.clone.1.owner_ref, s32[1]{0:T(128)} %constant.3.clone.1.length_ref, bf16[1,1,8,256,128]{4,3,2,1,0:T(8,128)(2,1)S(1)} %get-tuple-element.13.qk_ref, bf16[1,128,2048]{2,1,0:T(8,128)(2,1)S(1)} %copy-done, ...), custom_call_target="tpu_custom_call" | custom-call | tf_op jit(solution)/shard_map/sweep/pallas_call | solution.py:191
  116.7 0.0 copy-start.17
  116.7 0.0 copy-start.15
  116.7 0.0 copy-start.16
  116.7 0.0 copy-start.8
  116.7 0.0 copy-start.9
  116.7 1.1 broadcast_select_fusion
  117.8 0.0 all-reduce.2.cloned.1.call-update
  117.8 0.2 all-gather.2.cloned.1.call-start
  118.0 53.8 %all-reduce.2.cloned.1.call-done = f32[1,16,128,128]{3,2,1,0:T(8,128)} async-done(((f32[1,16,128,128]{3,2,1,0:T(8,128)}), f32[1,16,128,128]{3,2,1,0:T(8,128)}) %all-reduce.2.cloned.1.call-update) | async-done | bytes 1048592 | tf_op jit(solution)/shard_map/psum | solution.py:252
  171.8 0.0 all-gather.2.cloned.1.call-update
  171.8 0.0 copy-done.17
  171.8 0.2 fusion
  172.0 0.0 copy-done.15
  172.0 0.0 copy-done.16
  172.0 0.2 select_reduce_fusion
  172.2 0.0 copy-done.8
  172.2 0.0 copy-done.9
  172.2 0.0 copy-start.11
  172.3 1.2 copy-done.11
  173.5 0.0 copy-start.12
  173.5 1.2 copy-done.12
  174.7 0.0 copy-start.1
  174.7 21.7 %prepare.3 = (bf16[2,2,8,256,128]{4,3,2,1,0:T(8,128)(2,1)S(1)}, bf16[2,2,16,128,128]{4,3,2,1,0:T(8,128)(2,1)}, bf16[2,2,16,128,128]{4,3,2,1,0:T(8,128)(2,1)}) custom-call(bf16[2,256,1024]{2,1,0:T(8,128)(2,1)S(1)} %copy-done.11, bf16[2,256,1024]{2,1,0:T(8,128)(2,1)S(1)} %copy-done.12, f32[2,16,256]{2,1,0:T(8,128)S(1)} %copy-done.8, f32[2,16,256]{2,1,0:T(8,128)S(1)} %copy-done.9), custom_call_target="tpu_custom_call" | custom-call | flops 4026531840 | bytes 6553600 | tf_op jit(solution)/shard_map/prepare/pallas_call | solution.py:156
  196.4 0.0 copy-start.2
  196.4 1.3 copy-done.2
  197.7 0.0 all-gather.2.cloned.1.call-done.seed_ref
  197.7 0.0 copy-done.1
  197.7 0.0 copy-start.3
  197.7 1.6 copy-done.3
  199.3 18.9 %sweep.9 = bf16[2,256,2048]{2,1,0:T(8,128)(2,1)} custom-call(s32[2]{0:T(128)S(1)} %get-tuple-element.25.owner_ref, s32[2]{0:T(128)S(1)} %get-tuple-element.24.length_ref, bf16[2,2,8,256,128]{4,3,2,1,0:T(8,128)(2,1)S(1)} %copy-done.3, bf16[2,256,2048]{2,1,0:T(8,128)(2,1)S(1)} %copy-done.1, bf16[2,2,16,128,128]{4,3,2,1,0:T(8,128)(2,1)} %get-tuple-element.21.solve_ref, ...), custom_call_target="tpu_custom_call" | custom-call | tf_op jit(solution)/shard_map/sweep/pallas_call | solution.py:191
  (1 shorter events, 0.0 us)
Async XLA Ops:
  7.2 8.7 %copy-start = (bf16[1,128,2048]{2,1,0:T(8,128)(2,1)S(1)}, bf16[1,128,2048]{2,1,0:T(8,128)(2,1)}, u32[]{:S(2)}) copy-start(bf16[1,128,2048]{2,1,0:T(8,128)(2,1)} %v_ref.8) | copy-start | bytes 1572868
  7.2 164.6 %all-reduce.2.cloned.1.call-start = ((), (), s32[]{:S(2)}) async-start(), calls=%async_computation | async-start | bytes 2097152 | tf_op jit(solution)/shard_map/psum | solution.py:252
  7.2 0.7 copy-start.4
  8.0 0.7 copy-start.6
  8.7 0.9 copy-start.13
  9.6 0.9 copy-start.14
  10.6 5.3 %copy-start.5 = (f32[1,16,128]{2,1,0:T(8,128)S(1)}, f32[1,16,128]{2,1,0:T(8,128)}, u32[]{:S(2)}) copy-start(f32[1,16,128]{2,1,0:T(8,128)} %beta_ref.11) | copy-start | bytes 24580
  10.6 5.4 %copy-start.10 = (f32[128]{0:T(128)S(1)}, f32[128]{0:T(128)}, u32[]{:S(2)}) copy-start(f32[128]{0:T(128)} %param.24) | copy-start | bytes 1540
  21.4 27.3 %collective-permute-start = (f32[1,16,128,128]{3,2,1,0:T(8,128)S(1)}, f32[1,16,128,128]{3,2,1,0:T(8,128)S(1)}, u32[]{:S(2)}, u32[]{:S(2)}) collective-permute-start(f32[1,16,128,128]{3,2,1,0:T(8,128)S(1)} %get-tuple-element.16), channel_id=1, source_target_pairs={{0,4},{4,8},{8,12},{1,5},{5,9},{9,13},{2,6},{6,10},{10,14},{3,7},{... | collective-permute-start | bytes 3145736 | tf_op jit(solution)/shard_map/ppermute | solution.py:216
  54.3 56.9 %copy-start.7 = (f32[1,16,128]{2,1,0:T(8,128)S(1)}, f32[1,16,128]{2,1,0:T(8,128)}, u32[]{:S(2)}) copy-start(f32[1,16,128]{2,1,0:T(8,128)} %decay_ref.11) | copy-start | bytes 24580
  54.3 26.0 %collective-permute-start.1 = (f32[1,16,128,128]{3,2,1,0:T(8,128)S(1)}, f32[1,16,128,128]{3,2,1,0:T(8,128)S(1)}, u32[]{:S(2)}, u32[]{:S(2)}) collective-permute-start(f32[1,16,128,128]{3,2,1,0:T(8,128)S(1)} %get-tuple-element.17), channel_id=1, source_target_pairs={{0,4},{4,8},{8,12},{1,5},{5,9},{9,13},{2,6},{6,10},{10,14},{3,7},{... | collective-permute-start | bytes 3145736 | tf_op jit(solution)/shard_map/ppermute | solution.py:216
  85.9 25.3 %collective-permute-start.2 = (f32[1,16,128,128]{3,2,1,0:T(8,128)}, f32[1,16,128,128]{3,2,1,0:T(8,128)S(1)}, u32[]{:S(2)}, u32[]{:S(2)}) collective-permute-start(f32[1,16,128,128]{3,2,1,0:T(8,128)} %get-tuple-element.18), channel_id=1, source_target_pairs={{0,4},{4,8},{8,12},{1,5},{5,9},{9,13},{2,6},{6,10},{10,14},{3,7},{... | collective-permute-start | bytes 3145736 | tf_op jit(solution)/shard_map/ppermute | solution.py:216
  116.7 55.2 %copy-start.17 = (s32[16]{0:T(128)S(1)}, s32[16]{0:T(128)}, u32[]{:S(2)}) copy-start(s32[16]{0:T(128)} %param.25) | copy-start | bytes 196
  116.7 55.3 %copy-start.15 = (s32[16]{0:T(128)S(1)}, s32[16]{0:T(128)}, u32[]{:S(2)}) copy-start(s32[16]{0:T(128)} %param.26) | copy-start | bytes 196
  116.7 55.3 %copy-start.16 = (s32[16]{0:T(128)S(1)}, s32[16]{0:T(128)}, u32[]{:S(2)}) copy-start(s32[16]{0:T(128)} %param.27) | copy-start | bytes 196
  116.7 55.5 %copy-start.8 = (f32[2,16,256]{2,1,0:T(8,128)S(1)}, f32[2,16,256]{2,1,0:T(8,128)}, u32[]{:S(2)}) copy-start(f32[2,16,256]{2,1,0:T(8,128)} %beta_ref.13) | copy-start | bytes 98308
  116.7 55.5 %copy-start.9 = (f32[2,16,256]{2,1,0:T(8,128)S(1)}, f32[2,16,256]{2,1,0:T(8,128)}, u32[]{:S(2)}) copy-start(f32[2,16,256]{2,1,0:T(8,128)} %decay_ref.13) | copy-start | bytes 98308
  117.8 79.9 %all-gather.2.cloned.1.call-start = ((), (), s32[]{:S(2)}) async-start(), calls=%async_computation.1 | async-start | bytes 3145728 | tf_op jit(solution)/shard_map/all_gather | solution.py:253
  172.2 1.2 copy-start.11
  173.5 1.2 copy-start.12
  174.7 23.0 %copy-start.1 = (bf16[2,256,2048]{2,1,0:T(8,128)(2,1)S(1)}, bf16[2,256,2048]{2,1,0:T(8,128)(2,1)}, u32[]{:S(2)}) copy-start(bf16[2,256,2048]{2,1,0:T(8,128)(2,1)} %v_ref.9) | copy-start | bytes 6291460
  196.4 1.3 copy-start.2
  197.7 1.6 copy-start.3
Sparse Core Ops, SparseCore 0:
  117.9 53.8 all-reduce.1
  173.4 9.9 all-gather.1
where the time goes:
time: 225 us
  waiting for transfers between devices  118 us (52%)
  Pallas kernels  67.8 us (30%)
  starting transfers between devices  14.3 us (6%)
  between operations  14.2 us (6%)
  local copies, waits for them, and re-layouts  8.82 us (4%)
    ppermute x3, waiting for transfers between devices, from_behind(): return lax.ppermute(value, axis, [(i, i + 1) for i in range(count - 1)])  64.6 us
    psum x1, waiting for transfers between devices, local(): final = lax.psum(final, 'seq')  53.8 us
    pallas_call x5, Pallas kernels, sweep(): pl.pallas_call(functools.partial(seq_kernel, rep, keep), grid_spec=pltpu....  41 us
    pallas_call x2, Pallas kernels, prepare(): pl.pallas_call(functools.partial(pre_kernel, rep), grid=(slots, spans, ke...  26.9 us
    ppermute x3, starting transfers between devices, from_behind(): return lax.ppermute(value, axis, [(i, i + 1) for i in range(count - 1)])  14 us
    unnamed x36, local copies, waits for them, and re-layouts  8.73 us
  transfers between devices with their start and end apart: 5, of which 4 were waited for; matrix products, arithmetic and copies ran while one was open for 0% of the time, Pallas kernels for 10%

commit v1 on v0

--- a/solution.py
+++ b/solution.py
@@ -42,30 +42,33 @@
     )
 
 
-def pre_kernel(rep, q_ref, k_ref, beta_ref, decay_ref, qk_ref, solve_ref, gram_ref):
-    key_heads = q_ref.shape[2] // DK
-    heads = key_heads * rep
+def gate_columns(log_col, beta_col, j, rep):
+    hs = slice(j * rep, (j + 1) * rep)
+    return jnp.concatenate([log_col[:, hs], beta_col[:, hs]], axis=1)
+
+
+def gate_rows(log_row, beta_row, j, rep):
+    hs = slice(j * rep, (j + 1) * rep)
+    return jnp.concatenate([log_row[hs], beta_row[hs]], axis=0)
+
+
+def solve_spans(rep, queries, keys, gates_row, gates_col):
     rows, cols = iotas()
     upto = rows >= cols
     strict = rows > cols
     apart = rows ^ cols
-    log_row = running_log(decay_ref[0])
-    log_col = log_row.T
-    beta_row = beta_ref[0]
-    beta_col = beta_row.T
-    lower = []
-    for j in range(key_heads):
-        q = unit(q_ref[0, :, j * DK : (j + 1) * DK])
-        k = unit(k_ref[0, :, j * DK : (j + 1) * DK])
-        qk_ref[0, 0, j, :CH, :] = q
-        qk_ref[0, 0, j, CH:, :] = k
-        grams = mm(jnp.concatenate([q, k], axis=0), k, NT)
+    pairs, weights, lower = [], [], []
+    for q, k, row, col in zip(queries, keys, gates_row, gates_col):
+        q, k = unit(q), unit(k)
+        pair = jnp.concatenate([q, k], axis=0)
+        pairs.append(pair)
+        grams = mm(pair, k, NT)
         for r in range(rep):
-            h = j * rep + r
-            spread = log_col[:, h : h + 1] - log_row[h : h + 1, :]
+            spread = col[:, r : r + 1] - row[r : r + 1, :]
             ratio = jnp.exp(jnp.where(upto, spread, -1e30))
-            gram_ref[0, 0, h] = (grams[:CH] * ratio).astype(BF16)
-            lower.append(jnp.where(strict, beta_col[:, h : h + 1] * ratio * grams[CH:], 0.0))
+            weights.append((grams[:CH] * ratio).astype(BF16))
+            beta = col[:, rep + r : rep + r + 1]
+            lower.append(jnp.where(strict, beta * ratio * grams[CH:], 0.0))
     eye = jnp.where(rows == cols, 1.0, 0.0).astype(F32)
     first = strict & (apart == 1)
     inv = [eye - jnp.where(first, low, 0.0) for low in lower]
@@ -76,9 +79,35 @@
         mid = [mm(jnp.where(pick, low, 0.0).astype(BF16), t) for low, t in zip(lower, inv16)]
         inv = [t - mm(t16, x.astype(BF16)) for t, t16, x in zip(inv, inv16, mid)]
         level += 1
-    for h in range(heads):
-        off = jnp.where(strict, inv[h], 0.0) * beta_row[h : h + 1, :]
-        solve_ref[0, 0, h] = off.astype(BF16)
+    solves = []
+    for h, t in enumerate(inv):
+        row = gates_row[h // rep]
+        r = rep + h % rep
+        solves.append((jnp.where(strict, t, 0.0) * row[r : r + 1, :]).astype(BF16))
+    return pairs, weights, solves
+
+
+def pre_kernel(rep, q_ref, k_ref, beta_ref, decay_ref, qk_ref, solve_ref, gram_ref, cols_ref):
+    key_heads = q_ref.shape[2] // DK
+    log_row = running_log(decay_ref[0])
+    log_col = log_row.T
+    beta_row = beta_ref[0]
+    beta_col = beta_row.T
+    span = range(key_heads)
+    cols = [gate_columns(log_col, beta_col, j, rep) for j in span]
+    pairs, weights, solves = solve_spans(
+        rep,
+        [q_ref[0, :, j * DK : (j + 1) * DK] for j in span],
+        [k_ref[0, :, j * DK : (j + 1) * DK] for j in span],
+        [gate_rows(log_row, beta_row, j, rep) for j in span],
+        cols,
+    )
+    for j in span:
+        qk_ref[0, 0, j] = pairs[j]
+        cols_ref[0, 0, j] = cols[j]
+    for h in range(key_heads * rep):
+        gram_ref[0, 0, h] = weights[h]
+        solve_ref[0, 0, h] = solves[h]
 
 
 def advance(qk, vals, solve, gram, logs, beta_cols, states):
@@ -104,8 +133,8 @@
 
 
 def seq_kernel(
-    rep, keep, owner_ref, length_ref, qk_ref, v_ref, solve_ref, gram_ref,
-    beta_ref, decay_ref, seed_ref, gain_ref, out_ref, *end_ref
+    rep, owner_ref, length_ref, qk_ref, v_ref, solve_ref, gram_ref, cols_ref, seed_ref,
+    gain_ref, out_ref
 ):
     spans, key_heads = qk_ref.shape[1], qk_ref.shape[2]
     heads = key_heads * rep
@@ -115,18 +144,17 @@
     place = lax.broadcasted_iota(jnp.int32, (CH, DV), 0)
     for c in range(spans):
         span = slice(c * CH, (c + 1) * CH)
-        log_col = running_log(decay_ref[0, :, span]).T
-        beta_col = beta_ref[0, :, span].T
         live = place + c * CH < length
         for j in range(key_heads):
             hs = range(j * rep, (j + 1) * rep)
+            cols = cols_ref[0, c, j]
             outs, grown = advance(
                 qk_ref[0, c, j],
                 [v_ref[0, span, h * DV : (h + 1) * DV] for h in hs],
                 [solve_ref[0, c, h] for h in hs],
                 [gram_ref[0, c, h] for h in hs],
-                [log_col[:, h : h + 1] for h in hs],
-                [beta_col[:, h : h + 1] for h in hs],
+                [cols[:, r : r + 1] for r in range(rep)],
+                [cols[:, rep + r : rep + r + 1] for r in range(rep)],
                 [states[h] for h in hs],
             )
             for h, o, s in zip(hs, outs, grown):
@@ -134,9 +162,179 @@
                 out_ref[0, span, h * DV : (h + 1) * DV] = jnp.where(
                     live, norm_rows(o, gain), 0.0
                 ).astype(BF16)
-    if keep:
-        for h in range(heads):
-            end_ref[0][0, h] = states[h]
+
+
+def relay_kernel(
+    rep, pqk, pv, psolve, pgram, pcols, gain_ref, *rest
+):
+    if len(rest) == 10:
+        work, rest = None, rest
+    else:
+        work, rest = rest[:4] + rest[6:10] + rest[12:13], rest[4:6] + rest[10:12] + rest[13:]
+    pout, finals, inbox, outbox, fsend, frecv, bsend, brecv, csend, crecv = rest
+    key_heads = pqk.shape[2]
+    rank, last = lax.axis_index("seq"), lax.axis_size("seq") - 1
+    mine = lax.axis_index("prompt")
+    other = 1 - mine
+    gain = gain_ref[...]
+    items = 0
+    if work is not None:
+        sq, sk, sbeta, sdecay, sqk, ssolve, sgram, scols, srows = work
+        slots, spans = sqk.shape[0], sqk.shape[1]
+        pack = 2 if key_heads % 2 == 0 else 1
+        packs = key_heads // pack
+        items = slots * spans * packs
+
+    def forward(i):
+        return pltpu.make_async_remote_copy(
+            src_ref=outbox.at[i], dst_ref=inbox.at[i], send_sem=fsend.at[i],
+            recv_sem=frecv.at[i], device_id={"seq": rank + 1}, device_id_type=pl.DeviceIdType.MESH,
+        )
+
+    def block(p, i):
+        return finals.at[p, pl.ds(i * rep, rep)]
+
+    def backward(i):
+        return pltpu.make_async_remote_copy(
+            src_ref=block(mine, i), dst_ref=block(mine, i), send_sem=bsend.at[i],
+            recv_sem=brecv.at[i], device_id={"seq": rank - 1}, device_id_type=pl.DeviceIdType.MESH,
+        )
+
+    def across(p, i):
+        return pltpu.make_async_remote_copy(
+            src_ref=block(p, i), dst_ref=block(p, i), send_sem=csend.at[i],
+            recv_sem=crecv.at[i], device_id={"prompt": other}, device_id_type=pl.DeviceIdType.MESH,
+        )
+
+    barrier = pltpu.get_barrier_semaphore()
+
+    def greet(where):
+        pl.semaphore_signal(barrier, inc=1, device_id=where, device_id_type=pl.DeviceIdType.MESH)
+
+    greet({"prompt": other})
+
+    @pl.when(rank > 0)
+    def _():
+        greet({"seq": rank - 1})
+
+    @pl.when(rank < last)
+    def _():
+        greet({"seq": rank + 1})
+
+    pl.semaphore_wait(
+        barrier, 1 + jnp.where(rank > 0, 1, 0) + jnp.where(rank < last, 1, 0)
+    )
+
+    @pl.when(rank == 0)
+    def _():
+        inbox[...] = jnp.zeros_like(inbox)
+
+    if work is not None:
+        for s in range(slots):
+            for c in range(spans):
+                span = slice(c * CH, (c + 1) * CH)
+                log_row = running_log(sdecay[s, :, span])
+                beta_row = sbeta[s, :, span]
+                log_col, beta_col = log_row.T, beta_row.T
+                for j in range(key_heads):
+                    scols[s, c, j] = gate_columns(log_col, beta_col, j, rep)
+                    srows[s, c, j] = gate_rows(log_row, beta_row, j, rep)
+
+    def step_forward(i):
+        @pl.when(rank > 0)
+        def _():
+            forward(i).wait_recv()
+
+        at = pl.ds(pl.multiple_of(i * rep * DV, rep * DV), rep * DV)
+        v = pv[0, :, at]
+        cols = pcols[0, 0, i]
+        outs, grown = advance(
+            pqk[0, 0, i],
+            [v[:, r * DV : (r + 1) * DV] for r in range(rep)],
+            [psolve[0, 0, i * rep + r] for r in range(rep)],
+            [pgram[0, 0, i * rep + r] for r in range(rep)],
+            [cols[:, r : r + 1] for r in range(rep)],
+            [cols[:, rep + r : rep + r + 1] for r in range(rep)],
+            [inbox[i, r] for r in range(rep)],
+        )
+
+        @pl.when(rank < last)
+        def _():
+            for r in range(rep):
+                outbox[i, r] = grown[r]
+            forward(i).start()
+
+        @pl.when(rank == last)
+        def _():
+            for r in range(rep):
+                finals[mine, i * rep + r] = grown[r]
+
+        pout[0, :, at] = jnp.concatenate(
+            [norm_rows(o, gain).astype(BF16) for o in outs], axis=1
+        )
+
+    def step_back(i):
+        @pl.when(rank < last)
+        def _():
+            backward(i).wait_recv()
+
+        @pl.when(rank > 0)
+        def _():
+            backward(i).start()
+
+        across(mine, i).start()
+
+    def step_work(m):
+        place, g = m // packs, m % packs
+        s, c = place // spans, place % spans
+        rows = pl.ds(pl.multiple_of(c * CH, CH), CH)
+        at = pl.ds(pl.multiple_of(g * pack * DK, pack * DK), pack * DK)
+        q, k = sq[s, rows, at], sk[s, rows, at]
+        pairs, weights, solves = solve_spans(
+            rep,
+            [q[:, j * DK : (j + 1) * DK] for j in range(pack)],
+            [k[:, j * DK : (j + 1) * DK] for j in range(pack)],
+            [srows[s, c, g * pack + j] for j in range(pack)],
+            [scols[s, c, g * pack + j] for j in range(pack)],
+        )
+        for j in range(pack):
+            sqk[s, c, g * pack + j] = pairs[j]
+        for h in range(pack * rep):
+            sgram[s, c, g * pack * rep + h] = weights[h]
+            ssolve[s, c, g * pack * rep + h] = solves[h]
+
+    first_at = LAG * rank
+    back_at = LAG * last + (LAG + 1) * (last - rank)
+
+    def tick(t, carry):
+        i = t - first_at
+        pl.when((i >= 0) & (i < key_heads))(lambda: step_forward(i))
+        j = t - back_at
+        pl.when((j >= 0) & (j < key_heads))(lambda: step_back(j))
+        if work is not None:
+            pl.when(t < items)(lambda: step_work(t))
+        return carry
+
+    lax.fori_loop(0, max(items, (2 * LAG + 1) * last + key_heads), tick, 0)
+
+    def finish(i, carry):
+        @pl.when(rank < last)
+        def _():
+            forward(i).wait_send()
+
+        @pl.when(rank > 0)
+        def _():
+            backward(i).wait_send()
+
+        across(mine, i).wait_send()
+        across(other, i).wait_recv()
+        return carry
+
+    lax.fori_loop(0, key_heads, finish, 0)
+
+
+LAG = 2
+OVERLAP = True
 
 
 def group_of(key_heads):
@@ -161,11 +359,13 @@
             pl.BlockSpec((1, 1, g, 2 * CH, DK), lambda s, c, j: (s, c, j, 0, 0)),
             square,
             square,
+            pl.BlockSpec((1, 1, g, CH, 2 * rep), lambda s, c, j: (s, c, j, 0, 0)),
         ],
         out_shape=[
             jax.ShapeDtypeStruct((slots, spans, key_heads, 2 * CH, DK), BF16),
             jax.ShapeDtypeStruct((slots, spans, heads, CH, CH), BF16),
             jax.ShapeDtypeStruct((slots, spans, heads, CH, CH), BF16),
+            jax.ShapeDtypeStruct((slots, spans, key_heads, CH, 2 * rep), F32),
         ],
         compiler_params=pltpu.CompilerParams(**PARAMS),
         cost_estimate=pl.CostEstimate(
@@ -176,20 +376,55 @@
     )(q, k, beta, decay)
 
 
-def sweep(terms, v, beta, decay, seeds, owner, length, gain, keep):
-    qk, solve, gram = terms
+def relay(terms, v, gain, suffix):
+    key_heads, heads = terms[0].shape[2], terms[1].shape[2]
+    rep = heads // key_heads
+    count = lax.axis_size("prompt")
+    vmem = pl.BlockSpec(memory_space=pltpu.VMEM)
+    outs = [
+        jax.ShapeDtypeStruct(v.shape, BF16),
+        jax.ShapeDtypeStruct((count, heads, DK, DV), F32),
+    ]
+    scratch = [
+        pltpu.VMEM((key_heads, rep, DK, DV), F32),
+        pltpu.VMEM((key_heads, rep, DK, DV), F32),
+    ] + [pltpu.SemaphoreType.DMA((key_heads,))] * 6
+    args = [terms[0], v, terms[1], terms[2], terms[3], gain]
+    body = functools.partial(relay_kernel, rep)
+    if suffix is not None:
+        q, k, beta, decay = suffix
+        slots, spans = q.shape[0], q.shape[1] // CH
+        work_outs = [
+            jax.ShapeDtypeStruct((slots, spans, key_heads, 2 * CH, DK), BF16),
+            jax.ShapeDtypeStruct((slots, spans, heads, CH, CH), BF16),
+            jax.ShapeDtypeStruct((slots, spans, heads, CH, CH), BF16),
+            jax.ShapeDtypeStruct((slots, spans, key_heads, CH, 2 * rep), F32),
+        ]
+        args += list(suffix)
+        outs = outs + work_outs
+        scratch = scratch[:2] + [pltpu.VMEM((slots, spans, key_heads, 2 * rep, CH), F32)] + scratch[2:]
+    return pl.pallas_call(
+        body,
+        out_shape=outs,
+        in_specs=[vmem] * len(args),
+        out_specs=[vmem] * len(outs),
+        scratch_shapes=scratch,
+        compiler_params=pltpu.CompilerParams(
+            collective_id=0, has_side_effects=True, vmem_limit_bytes=56 * 1024 * 1024
+        ),
+        name="relay",
+    )(*args)
+
+
+def sweep(terms, v, seeds, owner, length, gain):
+    qk, solve, gram, cols = terms
     slots, spans, key_heads = qk.shape[:3]
-    heads = beta.shape[1]
+    heads = solve.shape[2]
     rep, g, tokens = heads // key_heads, group_of(key_heads), spans * CH
-    gate = pl.BlockSpec((1, g * rep, tokens), lambda s, j, *_: (s, j, 0))
     vals = pl.BlockSpec((1, tokens, g * rep * DV), lambda s, j, *_: (s, 0, j))
     square = pl.BlockSpec((1, spans, g * rep, CH, CH), lambda s, j, *_: (s, 0, j, 0, 0))
-    out_specs, out_shape = [vals], [jax.ShapeDtypeStruct(v.shape, BF16)]
-    if keep:
-        out_specs.append(pl.BlockSpec((1, g * rep, DK, DV), lambda s, j, *_: (s, j, 0, 0)))
-        out_shape.append(jax.ShapeDtypeStruct((slots, heads, DK, DV), F32))
     return pl.pallas_call(
-        functools.partial(seq_kernel, rep, keep),
+        functools.partial(seq_kernel, rep),
         grid_spec=pltpu.PrefetchScalarGridSpec(
             num_scalar_prefetch=2,
             grid=(slots, key_heads // g),
@@ -198,22 +433,16 @@
                 vals,
                 square,
                 square,
-                gate,
-                gate,
+                pl.BlockSpec((1, spans, g, CH, 2 * rep), lambda s, j, *_: (s, 0, j, 0, 0)),
                 pl.BlockSpec((1, g * rep, DK, DV), lambda s, j, own, _: (own[s], j, 0, 0)),
                 pl.BlockSpec((1, DV), lambda s, j, *_: (0, 0)),
             ],
-            out_specs=out_specs,
+            out_specs=vals,
         ),
-        out_shape=out_shape,
+        out_shape=jax.ShapeDtypeStruct(v.shape, BF16),
         compiler_params=pltpu.CompilerParams(**PARAMS),
         name="sweep",
-    )(owner, length, qk, v, solve, gram, beta, decay, seeds, gain)
-
-
-def from_behind(value, axis):
-    count = lax.axis_size(axis)
-    return lax.ppermute(value, axis, [(i, i + 1) for i in range(count - 1)])
+    )(owner, length, qk, v, solve, gram, cols, seeds, gain)
 
 
 def slot_facts(slot_branch, branch_length, branch_prompt, slot_count):
@@ -237,24 +466,13 @@
     gain = norm_gain[None, :]
     length, owner = slot_facts(slot_branch, branch_length, branch_prompt, suffix_queries.shape[0])
     terms = prepare(prompt_queries, prompt_keys, prompt_beta, prompt_decay)
-    heads = prompt_beta.shape[1]
-    whole = jnp.full((1,), prompt_queries.shape[1], jnp.int32)
-    zero = jnp.zeros((1,), jnp.int32)
-    state = jnp.zeros((1, heads, DK, DV), F32)
-    count = lax.axis_size("seq")
-    for step in range(count):
-        prompt_out, state_out = sweep(
-            terms, prompt_values, prompt_beta, prompt_decay, state, zero, whole, gain, True
-        )
-        if step < count - 1:
-            state = from_behind(state_out, "seq")
-    final = jnp.where(lax.axis_index("seq") == count - 1, state_out, 0.0)
-    final = lax.psum(final, "seq")
-    finals = lax.all_gather(final, "prompt", axis=0, tiled=True)
-    suffix_terms = prepare(suffix_queries, suffix_keys, suffix_beta, suffix_decay)
-    suffix_out = sweep(
-        suffix_terms, suffix_values, suffix_beta, suffix_decay, finals, owner, length, gain, False
-    )[0]
+    if OVERLAP:
+        suffix = (suffix_queries, suffix_keys, suffix_beta, suffix_decay)
+        prompt_out, finals, *suffix_terms = relay(terms, prompt_values, gain, suffix)
+    else:
+        prompt_out, finals = relay(terms, prompt_values, gain, None)
+        suffix_terms = prepare(suffix_queries, suffix_keys, suffix_beta, suffix_decay)
+    suffix_out = sweep(suffix_terms, suffix_values, finals, owner, length, gain)
     return (prompt_out, suffix_out)
 
 

time: 225 us -> 102 us (0.45)
  waiting for transfers between devices: 118 us -> 0 us
  Pallas kernels: 67.8 us -> 91.4 us
  starting transfers between devices: 14.3 us -> 0 us
  between operations: 14.2 us -> 0.73 us
    ppermute x3 -> x0, waiting for transfers between devices: 64.6 us -> none  [from_behind(): return lax.ppermute(value, axis, [(i, i + 1) for i in range(count - 1)])]
    psum x1 -> x0, waiting for transfers between devices: 53.8 us -> none  [local(): final = lax.psum(final, 'seq')]
    pallas_call x5 -> x2, Pallas kernels: 41 us -> 86 us  [the longest x1 67.8 us: relay(): pl.pallas_call(body, out_shape=outs, in_specs=[vmem] * len(args), out_spe...]
    pallas_call x2 -> x1, Pallas kernels: 26.9 us -> 5.46 us  [prepare(): pl.pallas_call(functools.partial(pre_kernel, rep), grid=(slots, spans, ke...]
    ppermute x3 -> x0, starting transfers between devices: 14 us -> none  [from_behind(): return lax.ppermute(value, axis, [(i, i + 1) for i in range(count - 1)])]
    unnamed x36 -> x31, local copies, waits for them, and re-layouts: 8.73 us -> 8.86 us
  transfers between devices with their start and end apart: 5 -> 0, of which waited for: 4 -> 0; matrix products, arithmetic and copies ran while one was open for 0% -> 0% of each run, Pallas kernels for 10% -> 0%
where the time goes in v1:
time: 102 us; the launch traced here: 101 us
  Pallas kernels  91.4 us (90%)
  local copies, waits for them, and re-layouts  8.86 us (9%)
    pallas_call x1, Pallas kernels, relay(): pl.pallas_call(body, out_shape=outs, in_specs=[vmem] * len(args), out_spe...  67.8 us
    pallas_call x1, Pallas kernels, sweep(): pl.pallas_call(functools.partial(seq_kernel, rep), grid_spec=pltpu.Prefet...  18.2 us
    unnamed x31, local copies, waits for them, and re-layouts  8.86 us
    pallas_call x1, Pallas kernels, prepare(): pl.pallas_call(functools.partial(pre_kernel, rep), grid=(slots, spans, ke...  5.46 us

profile of v1, /device:TPU:0, one launch (start us, length us, event | category | flops | bytes accessed | tf_op | source)
XLA Modules:
  0.0 101.4 jit_solution(1074552811923657287)
XLA Ops:
  0.6 0.0 copy-start.7
  0.6 0.9 copy-done.7
  1.6 0.0 copy-start.8
  1.6 0.9 copy-done.8
  2.5 0.0 copy-start.9
  2.5 0.7 copy-done.9
  3.2 0.0 copy-start.10
  3.2 0.7 copy-done.10
  3.9 5.5 %prepare.1 = (bf16[1,1,8,256,128]{4,3,2,1,0:T(8,128)(2,1)S(1)}, bf16[1,1,16,128,128]{4,3,2,1,0:T(8,128)(2,1)S(1)}, bf16[1,1,16,128,128]{4,3,2,1,0:T(8,128)(2,1)S(1)}, f32[1,1,8,128,4]{4,3,2,1,0:T(8,128)S(1)}) custom-call(bf16[1,128,1024]{2,1,0:T(8,128)(2,1)S(1)} %copy-done.7, bf16[1,128,1024]{2,1,0:T(8,128)(2,1)S(1)} %copy-done.8, ...), custom_call_target="tpu_custom_call" | custom-call | flops 1006632960 | bytes 1638400 | tf_op jit(solution)/shard_map/prepare/pallas_call | solution.py:354
  9.4 0.0 copy-start.2
  9.4 0.8 copy-done.2
  10.2 0.0 copy-start.3
  10.2 0.8 copy-done.3
  11.0 0.0 copy-start.4
  11.0 0.8 copy-done.4
  11.8 0.0 copy-start.5
  11.8 0.8 copy-done.5
  12.6 0.0 copy-start.14
  12.6 0.0 copy-start.12
  12.6 0.0 copy-start.13
  12.6 0.0 copy-start
  12.6 0.0 copy-start.6
  12.6 67.8 %relay.1 = (bf16[1,128,2048]{2,1,0:T(8,128)(2,1)}, f32[2,16,128,128]{3,2,1,0:T(8,128)}, bf16[2,2,8,256,128]{4,3,2,1,0:T(8,128)(2,1)}, bf16[2,2,16,128,128]{4,3,2...) custom-call(bf16[1,1,8,256,128]{4,3,2,1,0:T(8,128)(2,1)} %copy-done.2, ...), custom_call_target="tpu_custom_call" | custom-call | tf_op jit(solution)/shard_map/relay/pallas_call | solution.py:406
  80.4 0.0 copy-done.14
  80.5 0.2 fusion
  80.6 0.0 copy-done.12
  80.6 0.0 copy-done.13
  80.7 0.2 select_reduce_fusion
  80.8 0.0 copy-done
  80.8 0.0 copy-done.6
  80.9 0.0 copy-start.1
  80.9 1.6 %copy-done.1 = bf16[2,2,8,256,128]{4,3,2,1,0:T(8,128)(2,1)S(1)} copy-done((bf16[2,2,8,256,128]{4,3,2,1,0:T(8,128)(2,1)S(1)}, bf16[2,2,8,256,128]{4,3,2,1,0:T(8,128)(2,1)}, u32[]{:S(2)}) %copy-start.1) | copy-done | bytes 2097176
  82.4 0.0 copy-start.11
  82.4 18.2 %sweep.1 = bf16[2,256,2048]{2,1,0:T(8,128)(2,1)} custom-call(s32[2]{0:T(128)S(1)} %get-tuple-element.23.owner_ref, s32[2]{0:T(128)S(1)} %get-tuple-element.22.length_ref, bf16[2,2,8,256,128]{4,3,2,1,0:T(8,128)(2,1)S(1)} %copy-done.1, bf16[2,256,2048]{2,1,0:T(8,128)(2,1)S(1)} %copy-done, bf16[2,2,16,128,128]{4,3,2,1,0:T(8,128)(2,1)} %get-tuple-element.18.solve_ref, ...), custom_call_target="tpu_custom_call" | custom-call | tf_op jit(solution)/shard_map/sweep/pallas_call | solution.py:426
  100.6 0.0 copy-done.11
  100.6 0.8 copy.17
  (1 shorter events, 0.0 us)
Async XLA Ops:
  0.6 1.0 copy-start.7
  1.6 0.9 copy-start.8
  2.5 0.7 copy-start.9
  3.2 0.7 copy-start.10
  9.4 0.8 copy-start.2
  10.2 0.8 copy-start.3
  11.0 0.8 copy-start.4
  11.8 0.8 copy-start.5
  12.6 67.9 %copy-start.14 = (s32[16]{0:T(128)S(1)}, s32[16]{0:T(128)}, u32[]{:S(2)}) copy-start(s32[16]{0:T(128)} %param.25) | copy-start | bytes 196
  12.6 68.1 %copy-start.12 = (s32[16]{0:T(128)S(1)}, s32[16]{0:T(128)}, u32[]{:S(2)}) copy-start(s32[16]{0:T(128)} %param.26) | copy-start | bytes 196
  12.6 68.1 %copy-start.13 = (s32[16]{0:T(128)S(1)}, s32[16]{0:T(128)}, u32[]{:S(2)}) copy-start(s32[16]{0:T(128)} %param.27) | copy-start | bytes 196
  12.6 68.3 %copy-start = (bf16[2,256,2048]{2,1,0:T(8,128)(2,1)S(1)}, bf16[2,256,2048]{2,1,0:T(8,128)(2,1)}, u32[]{:S(2)}) copy-start(bf16[2,256,2048]{2,1,0:T(8,128)(2,1)} %v_ref.1) | copy-start | bytes 6291460
  12.6 68.3 %copy-start.6 = (f32[128]{0:T(128)S(1)}, f32[128]{0:T(128)}, u32[]{:S(2)}) copy-start(f32[128]{0:T(128)} %param.24) | copy-start | bytes 1540
  80.9 1.6 %copy-start.1 = (bf16[2,2,8,256,128]{4,3,2,1,0:T(8,128)(2,1)S(1)}, bf16[2,2,8,256,128]{4,3,2,1,0:T(8,128)(2,1)}, u32[]{:S(2)}) copy-start(bf16[2,2,8,256,128]{4,3,2,1,0:T(8,128)(2,1)} %get-tuple-element.17.qk_ref) | copy-start | bytes 6291460
  82.4 18.2 %copy-start.11 = (bf16[1,128,2048]{2,1,0:T(8,128)(2,1)S(1)}, bf16[1,128,2048]{2,1,0:T(8,128)(2,1)}, u32[]{:S(2)}) copy-start(bf16[1,128,2048]{2,1,0:T(8,128)(2,1)} %get-tuple-element.26) | copy-start | bytes 1572868

commit v2 on v1

--- a/solution.py
+++ b/solution.py
@@ -74,10 +74,34 @@
     inv = [eye - jnp.where(first, low, 0.0) for low in lower]
     level = 1
     while (1 << level) < CH:
+        size = 1 << level
         pick = strict & ((apart >> level) == 1)
         inv16 = [t.astype(BF16) for t in inv]
-        mid = [mm(jnp.where(pick, low, 0.0).astype(BF16), t) for low, t in zip(lower, inv16)]
-        inv = [t - mm(t16, x.astype(BF16)) for t, t16, x in zip(inv, inv16, mid)]
+        if size < HALF_FROM:
+            mid = [mm(jnp.where(pick, low, 0.0).astype(BF16), t) for low, t in zip(lower, inv16)]
+            inv = [t - mm(t16, x.astype(BF16)) for t, t16, x in zip(inv, inv16, mid)]
+        else:
+            starts = range(0, CH, 2 * size)
+
+            def odd(x):
+                return jnp.concatenate([x[i + size : i + 2 * size] for i in starts], axis=0)
+
+            def spread_odd(x, fill):
+                parts = []
+                for n, i in enumerate(starts):
+                    parts += [fill[i : i + size], x[n * size : (n + 1) * size]]
+                return jnp.concatenate(parts, axis=0)
+
+            blank = jnp.zeros((CH, CH), BF16)
+            chosen = odd(pick.astype(F32)) > 0
+            mid = [
+                mm(jnp.where(chosen, odd(low), 0.0).astype(BF16), t)
+                for low, t in zip(lower, inv16)
+            ]
+            inv = [
+                spread_odd(odd(t) - mm(odd(t16), spread_odd(x.astype(BF16), blank)), t)
+                for t, t16, x in zip(inv, inv16, mid)
+            ]
         level += 1
     solves = []
     for h, t in enumerate(inv):
@@ -110,20 +134,38 @@
         solve_ref[0, 0, h] = solves[h]
 
 
-def advance(qk, vals, solve, gram, logs, beta_cols, states):
-    reads = mm(qk, jnp.concatenate([s.astype(BF16) for s in states], axis=1))
-    outs, tails = [], []
-    for r, state in enumerate(states):
-        fade = jnp.exp(logs[r])
-        part = reads[:, r * DV : (r + 1) * DV]
-        resid = vals[r].astype(F32) - fade * part[CH:]
-        new = beta_cols[r] * resid + mm(solve[r], resid.astype(BF16))
-        outs.append(fade * part[:CH] + mm(gram[r], new.astype(BF16)))
-        tails.append((jnp.exp(logs[r][CH - 1 :, :] - logs[r]) * new).astype(BF16))
-    grown = mm(qk[CH:], jnp.concatenate(tails, axis=1), TN)
+def advance(rep, entries):
+    heads = [(n, r) for n in range(len(entries)) for r in range(rep)]
+    reads = [
+        mm(e[0], jnp.concatenate([s.astype(BF16) for s in e[5]], axis=1)) for e in entries
+    ]
+    fades = [jnp.exp(entries[n][4][:, r : r + 1]) for n, r in heads]
+    parts = [reads[n][:, r * DV : (r + 1) * DV] for n, r in heads]
+    resids = [
+        entries[n][1][r].astype(F32) - fade * part[CH:]
+        for (n, r), fade, part in zip(heads, fades, parts)
+    ]
+    news = [
+        entries[n][4][:, rep + r : rep + r + 1] * resid
+        + mm(entries[n][2][r], resid.astype(BF16))
+        for (n, r), resid in zip(heads, resids)
+    ]
+    ends = [entries[n][4][CH - 1 :, r : r + 1] for n, r in heads]
+    tails = [
+        (jnp.exp(end - entries[n][4][:, r : r + 1]) * new).astype(BF16)
+        for (n, r), end, new in zip(heads, ends, news)
+    ]
+    grown = [
+        mm(e[0][CH:], jnp.concatenate(tails[n * rep : (n + 1) * rep], axis=1), TN)
+        for n, e in enumerate(entries)
+    ]
     states = [
-        jnp.exp(logs[r][CH - 1 :, :]) * s + grown[:, r * DV : (r + 1) * DV]
-        for r, s in enumerate(states)
+        jnp.exp(end) * entries[n][5][r] + grown[n][:, r * DV : (r + 1) * DV]
+        for (n, r), end in zip(heads, ends)
+    ]
+    outs = [
+        fade * part[:CH] + mm(entries[n][3][r], new.astype(BF16))
+        for (n, r), fade, part, new in zip(heads, fades, parts, news)
     ]
     return outs, states
 
@@ -145,23 +187,24 @@
     for c in range(spans):
         span = slice(c * CH, (c + 1) * CH)
         live = place + c * CH < length
-        for j in range(key_heads):
-            hs = range(j * rep, (j + 1) * rep)
-            cols = cols_ref[0, c, j]
-            outs, grown = advance(
-                qk_ref[0, c, j],
-                [v_ref[0, span, h * DV : (h + 1) * DV] for h in hs],
-                [solve_ref[0, c, h] for h in hs],
-                [gram_ref[0, c, h] for h in hs],
-                [cols[:, r : r + 1] for r in range(rep)],
-                [cols[:, rep + r : rep + r + 1] for r in range(rep)],
-                [states[h] for h in hs],
-            )
-            for h, o, s in zip(hs, outs, grown):
-                states[h] = s
-                out_ref[0, span, h * DV : (h + 1) * DV] = jnp.where(
-                    live, norm_rows(o, gain), 0.0
-                ).astype(BF16)
+        outs, states = advance(
+            rep,
+            [
+                (
+                    qk_ref[0, c, j],
+                    [v_ref[0, span, h * DV : (h + 1) * DV] for h in range(j * rep, (j + 1) * rep)],
+                    [solve_ref[0, c, h] for h in range(j * rep, (j + 1) * rep)],
+                    [gram_ref[0, c, h] for h in range(j * rep, (j + 1) * rep)],
+                    cols_ref[0, c, j],
+                    states[j * rep : (j + 1) * rep],
+                )
+                for j in range(key_heads)
+            ],
+        )
+        for h, o in enumerate(outs):
+            out_ref[0, span, h * DV : (h + 1) * DV] = jnp.where(
+                live, norm_rows(o, gain), 0.0
+            ).astype(BF16)
 
 
 def relay_kernel(
@@ -181,7 +224,7 @@
     if work is not None:
         sq, sk, sbeta, sdecay, sqk, ssolve, sgram, scols, srows = work
         slots, spans = sqk.shape[0], sqk.shape[1]
-        pack = 2 if key_heads % 2 == 0 else 1
+        pack = PACK if key_heads % PACK == 0 else 1
         packs = key_heads // pack
         items = slots * spans * packs
 
@@ -249,13 +292,17 @@
         v = pv[0, :, at]
         cols = pcols[0, 0, i]
         outs, grown = advance(
-            pqk[0, 0, i],
-            [v[:, r * DV : (r + 1) * DV] for r in range(rep)],
-            [psolve[0, 0, i * rep + r] for r in range(rep)],
-            [pgram[0, 0, i * rep + r] for r in range(rep)],
-            [cols[:, r : r + 1] for r in range(rep)],
-            [cols[:, rep + r : rep + r + 1] for r in range(rep)],
-            [inbox[i, r] for r in range(rep)],
+            rep,
+            [
+                (
+                    pqk[0, 0, i],
+                    [v[:, r * DV : (r + 1) * DV] for r in range(rep)],
+                    [psolve[0, 0, i * rep + r] for r in range(rep)],
+                    [pgram[0, 0, i * rep + r] for r in range(rep)],
+                    cols,
+                    [inbox[i, r] for r in range(rep)],
+                )
+            ],
         )
 
         @pl.when(rank < last)
@@ -304,7 +351,7 @@
             ssolve[s, c, g * pack * rep + h] = solves[h]
 
     first_at = LAG * rank
-    back_at = LAG * last + (LAG + 1) * (last - rank)
+    back_at = LAG * last + BACK * (last - rank)
 
     def tick(t, carry):
         i = t - first_at
@@ -315,7 +362,7 @@
             pl.when(t < items)(lambda: step_work(t))
         return carry
 
-    lax.fori_loop(0, max(items, (2 * LAG + 1) * last + key_heads), tick, 0)
+    lax.fori_loop(0, max(items, (LAG + BACK) * last + key_heads), tick, 0)
 
     def finish(i, carry):
         @pl.when(rank < last)
@@ -333,7 +380,10 @@
     lax.fori_loop(0, key_heads, finish, 0)
 
 
-LAG = 2
+LAG = 1
+BACK = 2
+PACK = 2
+HALF_FROM = 16
 OVERLAP = True
 
 
@@ -341,7 +391,7 @@
     return 4 if key_heads % 4 == 0 else key_heads
 
 
-PARAMS = dict(vmem_limit_bytes=48 * 1024 * 1024)
+PARAMS = dict(vmem_limit_bytes=60 * 1024 * 1024)
 
 
 def prepare(q, k, beta, decay):

time: 102 us -> 81.9 us (0.80)
  Pallas kernels: 91.4 us -> 79.3 us
  local copies, waits for them, and re-layouts: 8.86 us -> 0.81 us
    unnamed x31 -> x9, local copies, waits for them, and re-layouts: 8.86 us -> 0.81 us
    pallas_call x1, Pallas kernels: 18.2 us -> 10.5 us  [sweep(): pl.pallas_call(functools.partial(seq_kernel, rep), grid_spec=pltpu.Prefet...]
    pallas_call x1, Pallas kernels: 67.8 us -> 61.7 us  [relay(): pl.pallas_call(body, out_shape=outs, in_specs=[vmem] * len(args), out_spe...]
    pallas_call x1, Pallas kernels: 5.46 us -> 7.07 us  [prepare(): pl.pallas_call(functools.partial(pre_kernel, rep), grid=(slots, spans, ke...]
where the time goes in v2:
time: 81.9 us; the launch traced here: 81.7 us
  Pallas kernels  79.3 us (97%)
  other arithmetic  0.88 us (1%)
    pallas_call x1, Pallas kernels, relay(): pl.pallas_call(body, out_shape=outs, in_specs=[vmem] * len(args), out_spe...  61.7 us
    pallas_call x1, Pallas kernels, sweep(): pl.pallas_call(functools.partial(seq_kernel, rep), grid_spec=pltpu.Prefet...  10.5 us
    pallas_call x1, Pallas kernels, prepare(): pl.pallas_call(functools.partial(pre_kernel, rep), grid=(slots, spans, ke...  7.07 us

profile of v2, /device:TPU:0, one launch (start us, length us, event | category | flops | bytes accessed | tf_op | source)
XLA Modules:
  0.0 81.7 jit_solution(4105787097546457112)
XLA Ops:
  0.6 7.1 %prepare.1 = (bf16[1,1,8,256,128]{4,3,2,1,0:T(8,128)(2,1)}, bf16[1,1,16,128,128]{4,3,2,1,0:T(8,128)(2,1)}, bf16[1,1,16,128,128]{4,3,2,1,0:T(8,128)(2,1)}, f32[1,1,8,128,4]{4,3,2,1,0:T(8,128)}) custom-call(bf16[1,128,1024]{2,1,0:T(8,128)(2,1)} %q_ref.1, bf16[1,128,1024]{2,1,0:T(8,128)(2,1)} %k_ref.1, f32[1,16,128]{2,1,0:T(8,128)} %beta_ref.1, ...), custom_call_target="tpu_custom_call" | custom-call | flops 1006632960 | bytes 1638400 | tf_op jit(solution)/shard_map/prepare/pallas_call | solution.py:404
  7.7 0.0 copy-start.3
  7.7 0.0 copy-start.1
  7.7 0.0 copy-start.2
  7.7 61.7 %relay.1 = (bf16[1,128,2048]{2,1,0:T(8,128)(2,1)}, f32[2,16,128,128]{3,2,1,0:T(8,128)}, bf16[2,2,8,256,128]{4,3,2,1,0:T(8,128)(2,1)}, bf16[2,2,16,128,128]{4,3,2...) custom-call(bf16[1,1,8,256,128]{4,3,2,1,0:T(8,128)(2,1)} %get-tuple-element.12.pqk, ...), custom_call_target="tpu_custom_call" | custom-call | tf_op jit(solution)/shard_map/relay/pallas_call | solution.py:456
  69.5 0.0 copy-done.3
  69.5 0.2 fusion
  69.7 0.0 copy-done.1
  69.7 0.0 copy-done.2
  69.7 0.7 select_reduce_fusion
  70.4 0.0 copy-start
  70.4 10.5 %sweep.1 = bf16[2,256,2048]{2,1,0:T(8,128)(2,1)} custom-call(s32[2]{0:T(128)} %get-tuple-element.23.owner_ref, s32[2]{0:T(128)} %get-tuple-element.22.length_ref, bf16[2,2,8,256,128]{4,3,2,1,0:T(8,128)(2,1)} %get-tuple-element.17.qk_ref, bf16[2,256,2048]{2,1,0:T(8,128)(2,1)} %v_ref.1, bf16[2,2,16,128,128]{4,3,2,1,0:T(8,128)(2,1)} %get-tuple-element.18.solve_ref, ...), custom_call_target="tpu_custom_call" | custom-call | tf_op jit(solution)/shard_map/sweep/pallas_call | solution.py:476
  80.9 0.0 copy-done
  80.9 0.8 copy.17
  (1 shorter events, 0.0 us)
Async XLA Ops:
  7.7 61.8 %copy-start.3 = (s32[16]{0:T(128)S(1)}, s32[16]{0:T(128)}, u32[]{:S(2)}) copy-start(s32[16]{0:T(128)} %param.25) | copy-start | bytes 196
  7.7 62.0 %copy-start.1 = (s32[16]{0:T(128)S(1)}, s32[16]{0:T(128)}, u32[]{:S(2)}) copy-start(s32[16]{0:T(128)} %param.26) | copy-start | bytes 196
  7.7 62.0 %copy-start.2 = (s32[16]{0:T(128)S(1)}, s32[16]{0:T(128)}, u32[]{:S(2)}) copy-start(s32[16]{0:T(128)} %param.27) | copy-start | bytes 196
  70.4 10.5 %copy-start = (bf16[1,128,2048]{2,1,0:T(8,128)(2,1)S(1)}, bf16[1,128,2048]{2,1,0:T(8,128)(2,1)}, u32[]{:S(2)}) copy-start(bf16[1,128,2048]{2,1,0:T(8,128)(2,1)} %get-tuple-element.26) | copy-start | bytes 1572868

commit v3 on v2

--- a/solution.py
+++ b/solution.py
@@ -272,7 +272,7 @@
     def _():
         inbox[...] = jnp.zeros_like(inbox)
 
-    if work is not None:
+    def fill_gates():
         for s in range(slots):
             for c in range(spans):
                 span = slice(c * CH, (c + 1) * CH)
@@ -356,6 +356,8 @@
     def tick(t, carry):
         i = t - first_at
         pl.when((i >= 0) & (i < key_heads))(lambda: step_forward(i))
+        if work is not None:
+            pl.when(t == 0)(fill_gates)
         j = t - back_at
         pl.when((j >= 0) & (j < key_heads))(lambda: step_back(j))
         if work is not None:
@@ -382,7 +384,7 @@
 
 LAG = 1
 BACK = 2
-PACK = 2
+PACK = 4
 HALF_FROM = 16
 OVERLAP = True
 

time: 81.9 us -> 81.8 us (level)
  no operation moved by 1% of the time
where the time goes in v3:
time: 81.8 us; the launch traced here: 81.6 us
  Pallas kernels  79.2 us (97%)
  other arithmetic  0.88 us (1%)
    pallas_call x1, Pallas kernels, relay(): pl.pallas_call(body, out_shape=outs, in_specs=[vmem] * len(args), out_spe...  61.6 us
    pallas_call x1, Pallas kernels, sweep(): pl.pallas_call(functools.partial(seq_kernel, rep), grid_spec=pltpu.Prefet...  10.5 us
    pallas_call x1, Pallas kernels, prepare(): pl.pallas_call(functools.partial(pre_kernel, rep), grid=(slots, spans, ke...  7.07 us

profile of v3, /device:TPU:0, one launch (start us, length us, event | category | flops | bytes accessed | tf_op | source)
XLA Modules:
  0.0 81.6 jit_solution(9083728162799999794)
XLA Ops:
  0.6 7.1 %prepare.1 = (bf16[1,1,8,256,128]{4,3,2,1,0:T(8,128)(2,1)}, bf16[1,1,16,128,128]{4,3,2,1,0:T(8,128)(2,1)}, bf16[1,1,16,128,128]{4,3,2,1,0:T(8,128)(2,1)}, f32[1,1,8,128,4]{4,3,2,1,0:T(8,128)}) custom-call(bf16[1,128,1024]{2,1,0:T(8,128)(2,1)} %q_ref.1, bf16[1,128,1024]{2,1,0:T(8,128)(2,1)} %k_ref.1, f32[1,16,128]{2,1,0:T(8,128)} %beta_ref.1, ...), custom_call_target="tpu_custom_call" | custom-call | flops 1006632960 | bytes 1638400 | tf_op jit(solution)/shard_map/prepare/pallas_call | solution.py:406
  7.7 0.0 copy-start.3
  7.7 0.0 copy-start.1
  7.7 0.0 copy-start.2
  7.7 61.6 %relay.1 = (bf16[1,128,2048]{2,1,0:T(8,128)(2,1)}, f32[2,16,128,128]{3,2,1,0:T(8,128)}, bf16[2,2,8,256,128]{4,3,2,1,0:T(8,128)(2,1)}, bf16[2,2,16,128,128]{4,3,2...) custom-call(bf16[1,1,8,256,128]{4,3,2,1,0:T(8,128)(2,1)} %get-tuple-element.12.pqk, ...), custom_call_target="tpu_custom_call" | custom-call | tf_op jit(solution)/shard_map/relay/pallas_call | solution.py:458
  69.4 0.0 copy-done.3
  69.4 0.2 fusion
  69.5 0.0 copy-done.1
  69.5 0.0 copy-done.2
  69.6 0.7 select_reduce_fusion
  70.3 0.0 copy-start
  70.3 10.5 %sweep.1 = bf16[2,256,2048]{2,1,0:T(8,128)(2,1)} custom-call(s32[2]{0:T(128)} %get-tuple-element.23.owner_ref, s32[2]{0:T(128)} %get-tuple-element.22.length_ref, bf16[2,2,8,256,128]{4,3,2,1,0:T(8,128)(2,1)} %get-tuple-element.17.qk_ref, bf16[2,256,2048]{2,1,0:T(8,128)(2,1)} %v_ref.1, bf16[2,2,16,128,128]{4,3,2,1,0:T(8,128)(2,1)} %get-tuple-element.18.solve_ref, ...), custom_call_target="tpu_custom_call" | custom-call | tf_op jit(solution)/shard_map/sweep/pallas_call | solution.py:478
  80.8 0.0 copy-done
  80.8 0.8 copy.17
  (1 shorter events, 0.0 us)
Async XLA Ops:
  7.7 61.7 %copy-start.3 = (s32[16]{0:T(128)S(1)}, s32[16]{0:T(128)}, u32[]{:S(2)}) copy-start(s32[16]{0:T(128)} %param.25) | copy-start | bytes 196
  7.7 61.8 %copy-start.1 = (s32[16]{0:T(128)S(1)}, s32[16]{0:T(128)}, u32[]{:S(2)}) copy-start(s32[16]{0:T(128)} %param.26) | copy-start | bytes 196
  7.7 61.8 %copy-start.2 = (s32[16]{0:T(128)S(1)}, s32[16]{0:T(128)}, u32[]{:S(2)}) copy-start(s32[16]{0:T(128)} %param.27) | copy-start | bytes 196
  70.3 10.5 %copy-start = (bf16[1,128,2048]{2,1,0:T(8,128)(2,1)S(1)}, bf16[1,128,2048]{2,1,0:T(8,128)(2,1)}, u32[]{:S(2)}) copy-start(bf16[1,128,2048]{2,1,0:T(8,128)(2,1)} %get-tuple-element.26) | copy-start | bytes 1572868
